TPU v7x, 256 devices: a whole 4x4x8 slice. The times are simulated.
256 devices in a mesh: hi: 8 (over y, core), lo: 32 (over x, z).
Axes of the slice: x: 4, y: 4, z: 8, core: 2. Of those that a mesh axis runs over, the one named last changes fastest.
Arguments:
- vectors: bfloat16 [128, 524288], P(None, ('hi', 'lo')), may hold values from -6 to 6
- leaves: bfloat16 [524288, 512], P(('hi', 'lo')), may hold values from -0.25 to 0.25
- u_local: bfloat16 [2, 524288, 128], P(None, ('hi', 'lo')), may hold values from -0.5 to 0.5
- v_local: bfloat16 [2, 524288, 128], P(None, ('hi', 'lo')), may hold values from -6 to 6
- u_upper: bfloat16 [8, 524288, 128], P(None, ('hi', 'lo')), may hold values from -0.5 to 0.5
- v_upper: bfloat16 [8, 524288, 128], P(None, ('hi', 'lo')), may hold values from -6 to 6
Outputs:
- krylov_last: bfloat16 [128, 524288], P(None, ('hi', 'lo'))
All inputs are finite; a program needn't handle non-finite values.
Results may differ from a plain program's by a relative error of at most 0.018.
Values sent between devices are 32-bit elements; how exact they have to be, the bound alone decides.
No kernel may reach another device: no remote copies, remote signals or barrier semaphores. Data moves between devices by JAX's collectives and lax.ppermute only.
A program may use at most 64 MiB of HBM per device.

v0:
```python
import math

import jax
import jax.numpy as jnp
from jax import lax
from jax.sharding import PartitionSpec as P

ITERS = 4


def from_partner(value, axis, distance):
    mask = 2**distance
    pairs = [(source, source ^ mask) for source in range(lax.axis_size(axis))]
    return lax.ppermute(value, axis, pairs)


def lower_steps(stack, lo_bits):
    found = []
    carried = stack
    for level_bit in range(lo_bits):
        arrived = from_partner(carried, "lo", level_bit)
        found.append(arrived[0])
        carried = carried[1:] + arrived[1:]
    return (found, carried)


def upper_sums(hi_parts, hi_bits):
    found = []
    carried = hi_parts
    for level_bit in range(hi_bits):
        arrived = from_partner(carried, "hi", level_bit)
        found.append(arrived[0])
        carried = carried[1:] + arrived[1:]
    return found


def apply_operator(state, leaves, u_local, v_local, u_upper, v_upper):
    wide, dev_rows = state.shape
    leaf_rows = leaves.shape[1]
    local_count = u_local.shape[0]
    upper_count = u_upper.shape[0]
    level_count = local_count + upper_count
    lo_bits = lax.axis_size("lo").bit_length() - 1
    hi_bits = lax.axis_size("hi").bit_length() - 1
    rank_cols = u_local.shape[2]
    parts = jnp.einsum("bsr,cs->bcr", v_upper, state, preferred_element_type=jnp.float32)
    lower_found, hi_parts = lower_steps(parts, lo_bits)
    blocks = leaves.reshape(dev_rows // leaf_rows, leaf_rows, leaf_rows)
    result = jnp.einsum(
        "gij,cgj->cgi",
        blocks,
        state.reshape(wide, dev_rows // leaf_rows, leaf_rows),
        preferred_element_type=jnp.float32,
    ).reshape(wide, dev_rows)
    for level in range(local_count):
        node_rows = leaf_rows * 2**level
        groups = dev_rows // node_rows
        coef = jnp.einsum(
            "gsr,cgs->gcr",
            v_local[level].reshape(groups, node_rows, rank_cols),
            state.reshape(wide, groups, node_rows),
            preferred_element_type=jnp.float32,
        )
        coef = coef.reshape(groups // 2, 2, wide, rank_cols)[:, ::-1].reshape(
            groups, wide, rank_cols
        )
        coef = (coef * (1.0 / math.sqrt(node_rows * level_count))).astype(jnp.bfloat16)
        added = jnp.einsum(
            "gsr,gcr->cgs",
            u_local[level].reshape(groups, node_rows, rank_cols),
            coef,
            preferred_element_type=jnp.float32,
        )
        result = result + added.reshape(wide, dev_rows)
    upper_found = upper_sums(hi_parts, hi_bits)
    coefs = jnp.stack(lower_found + upper_found)
    factors = jnp.array(
        [
            1.0 / math.sqrt(dev_rows * 2**level_bit * level_count)
            for level_bit in range(upper_count)
        ],
        dtype=jnp.float32,
    )
    coefs = (coefs * factors[:, None, None]).astype(jnp.bfloat16)
    result = result + jnp.einsum("bsr,bcr->cs", u_upper, coefs, preferred_element_type=jnp.float32)
    return result.astype(jnp.bfloat16)


def local(vectors, leaves, u_local, v_local, u_upper, v_upper):
    state = vectors
    for step in range(ITERS):
        state = apply_operator(state, leaves, u_local, v_local, u_upper, v_upper)
    return state


def solution(mesh):
    return jax.shard_map(
        local,
        mesh=mesh,
        in_specs=(
            P(None, ("hi", "lo")),
            P(("hi", "lo"), None),
            P(None, ("hi", "lo"), None),
            P(None, ("hi", "lo"), None),
            P(None, ("hi", "lo"), None),
            P(None, ("hi", "lo"), None),
        ),
        out_specs=P(None, ("hi", "lo")),
        check_vma=False,
    )
```

profile of v0, /device:TPU:6, one launch (start us, length us, event | category | flops | bytes accessed | tf_op | source)
XLA Modules:
  0.0 416.3 jit_solution(10217327151187016802)
XLA Ops:
  0.0 3.2 convolution_bitcast_fusion.11
  3.2 2.0 collective-permute-start
  6.9 10.2 %collective-permute-done = f32[8,128,128]{2,1,0:T(8,128)S(1)} collective-permute-done((f32[8,128,128]{2,1,0:T(8,128)S(1)}, f32[8,128,128]{2,1,0:T(8,128)S(1)}, u32[]{:S(2)}, u32[]{:S(2)}) %collective-permute-start) | collective-permute-done | bytes 524320 | tf_op jit(solution)/shard_map/ppermute | solution.py:14
  17.2 3.4 collective-permute-start.1
  20.7 19.6 %collective-permute-done.1 = f32[7,128,128]{2,1,0:T(8,128)S(1)} collective-permute-done((f32[7,128,128]{2,1,0:T(8,128)S(1)}, f32[7,128,128]{2,1,0:T(8,128)S(1)}, u32[]{:S(2)}, u32[]{:S(2)}) %collective-permute-start.1) | collective-permute-done | bytes 458784 | tf_op jit(solution)/shard_map/ppermute | solution.py:14
  40.3 6.3 %collective-permute-start.2 = (f32[6,128,128]{2,1,0:T(8,128)S(1)}, f32[6,128,128]{2,1,0:T(8,128)S(1)}, u32[]{:S(2)}, u32[]{:S(2)}) collective-permute-start(f32[6,128,128]{2,1,0:T(8,128)S(1)} %slice_add_fusion.7), channel_id=1, source_target_pairs={{0,4},{1,5},{2,6},{3,7},{4,0},{5,1},{6,2},{7,3},{8,12},{9,13},{10,... | collective-permute-start | bytes 1179656 | tf_op jit(solution)/shard_map/ppermute | solution.py:14
  46.6 1.3 fusion.11
  47.9 16.0 %collective-permute-done.2 = f32[6,128,128]{2,1,0:T(8,128)S(1)} collective-permute-done((f32[6,128,128]{2,1,0:T(8,128)S(1)}, f32[6,128,128]{2,1,0:T(8,128)S(1)}, u32[]{:S(2)}, u32[]{:S(2)}) %collective-permute-start.2) | collective-permute-done | bytes 393248 | tf_op jit(solution)/shard_map/ppermute | solution.py:14
  66.1 6.4 %collective-permute-done.3 = f32[5,128,128]{2,1,0:T(8,128)S(1)} collective-permute-done((f32[5,128,128]{2,1,0:T(8,128)S(1)}, f32[5,128,128]{2,1,0:T(8,128)S(1)}, u32[]{:S(2)}, u32[]{:S(2)}) %collective-permute-start.3) | collective-permute-done | bytes 327712 | tf_op jit(solution)/shard_map/ppermute | solution.py:14
  72.5 1.5 collective-permute-start.4
  75.2 5.2 %collective-permute-done.4 = f32[4,128,128]{2,1,0:T(8,128)S(1)} collective-permute-done((f32[4,128,128]{2,1,0:T(8,128)S(1)}, f32[4,128,128]{2,1,0:T(8,128)S(1)}, u32[]{:S(2)}, u32[]{:S(2)}) %collective-permute-start.4) | collective-permute-done | bytes 262176 | tf_op jit(solution)/shard_map/ppermute | solution.py:14
  82.0 1.7 collective-permute-start.6
  84.4 3.3 collective-permute-done.6
  88.3 3.2 collective-permute-start.7
  92.8 2.5 copy.21
  95.3 2.6 copy.23
  97.9 2.5 copy.22
  100.4 2.5 copy.24
  103.6 4.8 %fusion.7 = bf16[128,2048]{1,0:T(8,128)(2,1)S(1)} fusion(bf16[8,2048,128]{2,1,0:T(8,128)(2,1)} %param.14, f32[128,2048]{1,0:T(8,128)} %copy.23, f32[128,2048]{1,0:T(8,128)} %copy.24, f32[8,128,128]{2,1,0:T(8,128)} %constant_dynamic-update-slice_fusion, f32[8]{0:T(128)S(1)} %copy-done.15), kind=kOutput, calls=%fused_computation.11 | convolution fusion | flops 537919488 | bytes 7340064 | tf_op jit(solution)/shard_map/bsr,bcr->cs/dot_general | solution.py:85
  109.5 12.5 %collective-permute-done.8 = f32[8,128,128]{2,1,0:T(8,128)S(1)} collective-permute-done((f32[8,128,128]{2,1,0:T(8,128)S(1)}, f32[8,128,128]{2,1,0:T(8,128)S(1)}, u32[]{:S(2)}, u32[]{:S(2)}) %collective-permute-start.8) | collective-permute-done | bytes 524320 | tf_op jit(solution)/shard_map/ppermute | solution.py:14
  122.1 3.1 collective-permute-start.9
  126.4 17.8 %collective-permute-done.9 = f32[7,128,128]{2,1,0:T(8,128)S(1)} collective-permute-done((f32[7,128,128]{2,1,0:T(8,128)S(1)}, f32[7,128,128]{2,1,0:T(8,128)S(1)}, u32[]{:S(2)}, u32[]{:S(2)}) %collective-permute-start.9) | collective-permute-done | bytes 458784 | tf_op jit(solution)/shard_map/ppermute | solution.py:14
  144.2 4.2 %collective-permute-start.10 = (f32[6,128,128]{2,1,0:T(8,128)S(1)}, f32[6,128,128]{2,1,0:T(8,128)S(1)}, u32[]{:S(2)}, u32[]{:S(2)}) collective-permute-start(f32[6,128,128]{2,1,0:T(8,128)S(1)} %slice_add_fusion.6), channel_id=1, source_target_pairs={{0,4},{1,5},{2,6},{3,7},{4,0},{5,1},{6,2},{7,3},{8,12},{9,13},{10,... | collective-permute-start | bytes 1179656 | tf_op jit(solution)/shard_map/ppermute | solution.py:14
  148.4 1.3 fusion.10
  149.7 17.1 %collective-permute-done.10 = f32[6,128,128]{2,1,0:T(8,128)S(1)} collective-permute-done((f32[6,128,128]{2,1,0:T(8,128)S(1)}, f32[6,128,128]{2,1,0:T(8,128)S(1)}, u32[]{:S(2)}, u32[]{:S(2)}) %collective-permute-start.10) | collective-permute-done | bytes 393248 | tf_op jit(solution)/shard_map/ppermute | solution.py:14
  169.1 6.9 %collective-permute-done.11 = f32[5,128,128]{2,1,0:T(8,128)S(1)} collective-permute-done((f32[5,128,128]{2,1,0:T(8,128)S(1)}, f32[5,128,128]{2,1,0:T(8,128)S(1)}, u32[]{:S(2)}, u32[]{:S(2)}) %collective-permute-start.11) | collective-permute-done | bytes 327712 | tf_op jit(solution)/shard_map/ppermute | solution.py:14
  176.0 1.4 collective-permute-start.12
  178.7 5.6 %collective-permute-done.12 = f32[4,128,128]{2,1,0:T(8,128)S(1)} collective-permute-done((f32[4,128,128]{2,1,0:T(8,128)S(1)}, f32[4,128,128]{2,1,0:T(8,128)S(1)}, u32[]{:S(2)}, u32[]{:S(2)}) %collective-permute-start.12) | collective-permute-done | bytes 262176 | tf_op jit(solution)/shard_map/ppermute | solution.py:14
  187.2 4.3 %collective-permute-done.14 = f32[2,128,128]{2,1,0:T(8,128)S(1)} collective-permute-done((f32[2,128,128]{2,1,0:T(8,128)S(1)}, f32[2,128,128]{2,1,0:T(8,128)S(1)}, u32[]{:S(2)}, u32[]{:S(2)}) %collective-permute-start.14) | collective-permute-done | bytes 131104 | tf_op jit(solution)/shard_map/ppermute | solution.py:14
  194.2 2.5 copy.28
  196.8 2.5 copy.30
  199.3 2.5 copy.27
  201.8 2.6 copy.29
  205.0 4.8 %fusion.6 = bf16[128,2048]{1,0:T(8,128)(2,1)S(1)} fusion(bf16[8,2048,128]{2,1,0:T(8,128)(2,1)} %param.14, f32[128,2048]{1,0:T(8,128)} %copy.29, f32[128,2048]{1,0:T(8,128)} %copy.30, f32[8,128,128]{2,1,0:T(8,128)} %constant_dynamic-update-slice_fusion.8, f32[8]{0:T(128)S(1)} %copy-done.15), kind=kOutput, calls=%fused_computation.10 | convolution fusion | flops 537919488 | bytes 7340064 | tf_op jit(solution)/shard_map/bsr,bcr->cs/dot_general | solution.py:85
  210.9 12.9 %collective-permute-done.16 = f32[8,128,128]{2,1,0:T(8,128)S(1)} collective-permute-done((f32[8,128,128]{2,1,0:T(8,128)S(1)}, f32[8,128,128]{2,1,0:T(8,128)S(1)}, u32[]{:S(2)}, u32[]{:S(2)}) %collective-permute-start.16) | collective-permute-done | bytes 524320 | tf_op jit(solution)/shard_map/ppermute | solution.py:14
  223.9 3.5 collective-permute-start.17
  228.5 18.1 %collective-permute-done.17 = f32[7,128,128]{2,1,0:T(8,128)S(1)} collective-permute-done((f32[7,128,128]{2,1,0:T(8,128)S(1)}, f32[7,128,128]{2,1,0:T(8,128)S(1)}, u32[]{:S(2)}, u32[]{:S(2)}) %collective-permute-start.17) | collective-permute-done | bytes 458784 | tf_op jit(solution)/shard_map/ppermute | solution.py:14
  246.6 3.9 collective-permute-start.18
  251.8 17.3 %collective-permute-done.18 = f32[6,128,128]{2,1,0:T(8,128)S(1)} collective-permute-done((f32[6,128,128]{2,1,0:T(8,128)S(1)}, f32[6,128,128]{2,1,0:T(8,128)S(1)}, u32[]{:S(2)}, u32[]{:S(2)}) %collective-permute-start.18) | collective-permute-done | bytes 393248 | tf_op jit(solution)/shard_map/ppermute | solution.py:14
  271.3 7.1 %collective-permute-done.19 = f32[5,128,128]{2,1,0:T(8,128)S(1)} collective-permute-done((f32[5,128,128]{2,1,0:T(8,128)S(1)}, f32[5,128,128]{2,1,0:T(8,128)S(1)}, u32[]{:S(2)}, u32[]{:S(2)}) %collective-permute-start.19) | collective-permute-done | bytes 327712 | tf_op jit(solution)/shard_map/ppermute | solution.py:14
  278.5 1.3 collective-permute-start.20
  281.1 5.8 %collective-permute-done.20 = f32[4,128,128]{2,1,0:T(8,128)S(1)} collective-permute-done((f32[4,128,128]{2,1,0:T(8,128)S(1)}, f32[4,128,128]{2,1,0:T(8,128)S(1)}, u32[]{:S(2)}, u32[]{:S(2)}) %collective-permute-start.20) | collective-permute-done | bytes 262176 | tf_op jit(solution)/shard_map/ppermute | solution.py:14
  289.6 4.5 %collective-permute-done.22 = f32[2,128,128]{2,1,0:T(8,128)S(1)} collective-permute-done((f32[2,128,128]{2,1,0:T(8,128)S(1)}, f32[2,128,128]{2,1,0:T(8,128)S(1)}, u32[]{:S(2)}, u32[]{:S(2)}) %collective-permute-start.22) | collective-permute-done | bytes 131104 | tf_op jit(solution)/shard_map/ppermute | solution.py:14
  294.7 2.2 collective-permute-start.23
  298.2 2.5 copy.34
  300.7 2.5 copy.36
  303.2 2.5 copy.33
  305.8 2.6 copy.35
  309.0 4.8 %fusion.5 = bf16[128,2048]{1,0:T(8,128)(2,1)S(1)} fusion(bf16[8,2048,128]{2,1,0:T(8,128)(2,1)} %param.14, f32[128,2048]{1,0:T(8,128)} %copy.35, f32[128,2048]{1,0:T(8,128)} %copy.36, f32[8,128,128]{2,1,0:T(8,128)} %constant_dynamic-update-slice_fusion.16, f32[8]{0:T(128)S(1)} %copy-done.15), kind=kOutput, calls=%fused_computation.9 | convolution fusion | flops 537919488 | bytes 7340064 | tf_op jit(solution)/shard_map/bsr,bcr->cs/dot_general | solution.py:85
  314.9 12.5 %collective-permute-done.24 = f32[8,128,128]{2,1,0:T(8,128)S(1)} collective-permute-done((f32[8,128,128]{2,1,0:T(8,128)S(1)}, f32[8,128,128]{2,1,0:T(8,128)S(1)}, u32[]{:S(2)}, u32[]{:S(2)}) %collective-permute-start.24) | collective-permute-done | bytes 524320 | tf_op jit(solution)/shard_map/ppermute | solution.py:14
  327.5 3.5 collective-permute-start.25
  332.2 17.7 %collective-permute-done.25 = f32[7,128,128]{2,1,0:T(8,128)S(1)} collective-permute-done((f32[7,128,128]{2,1,0:T(8,128)S(1)}, f32[7,128,128]{2,1,0:T(8,128)S(1)}, u32[]{:S(2)}, u32[]{:S(2)}) %collective-permute-start.25) | collective-permute-done | bytes 458784 | tf_op jit(solution)/shard_map/ppermute | solution.py:14
  350.0 3.5 collective-permute-start.26
  353.5 1.3 fusion.8
  354.8 17.7 %collective-permute-done.26 = f32[6,128,128]{2,1,0:T(8,128)S(1)} collective-permute-done((f32[6,128,128]{2,1,0:T(8,128)S(1)}, f32[6,128,128]{2,1,0:T(8,128)S(1)}, u32[]{:S(2)}, u32[]{:S(2)}) %collective-permute-start.26) | collective-permute-done | bytes 393248 | tf_op jit(solution)/shard_map/ppermute | solution.py:14
  373.3 8.9 %collective-permute-done.27 = f32[5,128,128]{2,1,0:T(8,128)S(1)} collective-permute-done((f32[5,128,128]{2,1,0:T(8,128)S(1)}, f32[5,128,128]{2,1,0:T(8,128)S(1)}, u32[]{:S(2)}, u32[]{:S(2)}) %collective-permute-start.27) | collective-permute-done | bytes 327712 | tf_op jit(solution)/shard_map/ppermute | solution.py:14
  383.4 7.9 %collective-permute-done.28 = f32[4,128,128]{2,1,0:T(8,128)S(1)} collective-permute-done((f32[4,128,128]{2,1,0:T(8,128)S(1)}, f32[4,128,128]{2,1,0:T(8,128)S(1)}, u32[]{:S(2)}, u32[]{:S(2)}) %collective-permute-start.28) | collective-permute-done | bytes 262176 | tf_op jit(solution)/shard_map/ppermute | solution.py:14
  391.4 1.4 collective-permute-done.29
  393.2 5.2 %collective-permute-done.30 = f32[2,128,128]{2,1,0:T(8,128)S(1)} collective-permute-done((f32[2,128,128]{2,1,0:T(8,128)S(1)}, f32[2,128,128]{2,1,0:T(8,128)S(1)}, u32[]{:S(2)}, u32[]{:S(2)}) %collective-permute-start.30) | collective-permute-done | bytes 131104 | tf_op jit(solution)/shard_map/ppermute | solution.py:14
  401.0 2.5 copy.40
  403.6 2.5 copy.42
  406.1 2.5 copy.39
  408.6 2.6 copy.41
  411.2 5.1 %fusion.4 = bf16[128,2048]{1,0:T(8,128)(2,1)} fusion(bf16[8,2048,128]{2,1,0:T(8,128)(2,1)} %param.14, f32[128,2048]{1,0:T(8,128)} %copy.41, f32[128,2048]{1,0:T(8,128)} %copy.42, f32[8,128,128]{2,1,0:T(8,128)S(1)} %constant_dynamic-update-slice_fusion.24, f32[8]{0:T(128)S(1)} %copy-done.15), kind=kOutput, calls=%fused_computation.8 | convolution fusion | flops 537919488 | bytes 7340064 | tf_op jit(solution)/shard_map/bsr,bcr->cs/dot_general | solution.py:85
  (142 shorter events, 42.0 us)
Async XLA Ops:
  0.0 6.1 %copy-start = (bf16[2048,512]{1,0:T(8,128)(2,1)S(1)}, bf16[2048,512]{1,0:T(8,128)(2,1)}, u32[]{:S(2)}) copy-start(bf16[2048,512]{1,0:T(8,128)(2,1)} %param.11) | copy-start | bytes 6291460
  0.0 5.3 %copy-start.8 = (bf16[128,2048]{1,0:T(8,128)(2,1)S(1)}, bf16[128,2048]{1,0:T(8,128)(2,1)}, u32[]{:S(2)}) copy-start(bf16[128,2048]{1,0:T(8,128)(2,1)} %param.10) | copy-start | bytes 1572868
  0.0 5.2 %copy-start.9 = (bf16[2,2048,128]{2,1,0:T(8,128)(2,1)S(1)}, bf16[2,2048,128]{2,1,0:T(8,128)(2,1)}, u32[]{:S(2)}) copy-start(bf16[2,2048,128]{2,1,0:T(8,128)(2,1)} %param.13) | copy-start | bytes 3145732
  3.2 13.9 %collective-permute-start = (f32[8,128,128]{2,1,0:T(8,128)S(1)}, f32[8,128,128]{2,1,0:T(8,128)S(1)}, u32[]{:S(2)}, u32[]{:S(2)}) collective-permute-start(f32[8,128,128]{2,1,0:T(8,128)S(1)} %convolution_bitcast_fusion.11), channel_id=1, source_target_pairs={{0,1},{1,0},{2,3},{3,2},{4,5},{5,4},{6,7},{7,6},{8,9},{9,8},{10,11... | collective-permute-start | bytes 1572872 | tf_op jit(solution)/shard_map/ppermute | solution.py:14
  5.3 0.8 copy-start.11
  5.3 15.3 %copy-start.10 = (bf16[2,2048,128]{2,1,0:T(8,128)(2,1)S(1)}, bf16[2,2048,128]{2,1,0:T(8,128)(2,1)}, u32[]{:S(2)}) copy-start(bf16[2,2048,128]{2,1,0:T(8,128)(2,1)} %param.12) | copy-start | bytes 3145732
  17.2 23.0 %collective-permute-start.1 = (f32[7,128,128]{2,1,0:T(8,128)S(1)}, f32[7,128,128]{2,1,0:T(8,128)S(1)}, u32[]{:S(2)}, u32[]{:S(2)}) collective-permute-start(f32[7,128,128]{2,1,0:T(8,128)S(1)} %slice_add_fusion.3), channel_id=1, source_target_pairs={{0,2},{1,3},{2,0},{3,1},{4,6},{5,7},{6,4},{7,5},{8,10},{9,11},{10,... | collective-permute-start | bytes 1376264 | tf_op jit(solution)/shard_map/ppermute | solution.py:14
  20.7 25.9 %copy-start.4 = (bf16[1,2048,128]{2,1,0:T(8,128)(2,1)}, bf16[1,2048,128]{2,1,0:T(8,128)(2,1)S(1)}, u32[]{:S(2)}) copy-start(bf16[1,2048,128]{2,1,0:T(8,128)(2,1)S(1)} %get-tuple-element.6) | copy-start | bytes 1572868
  40.3 23.6 %collective-permute-start.2 = (f32[6,128,128]{2,1,0:T(8,128)S(1)}, f32[6,128,128]{2,1,0:T(8,128)S(1)}, u32[]{:S(2)}, u32[]{:S(2)}) collective-permute-start(f32[6,128,128]{2,1,0:T(8,128)S(1)} %slice_add_fusion.7), channel_id=1, source_target_pairs={{0,4},{1,5},{2,6},{3,7},{4,0},{5,1},{6,2},{7,3},{8,12},{9,13},{10,... | collective-permute-start | bytes 1179656 | tf_op jit(solution)/shard_map/ppermute | solution.py:14
  63.9 8.5 %collective-permute-start.3 = (f32[5,128,128]{2,1,0:T(8,128)S(1)}, f32[5,128,128]{2,1,0:T(8,128)S(1)}, u32[]{:S(2)}, u32[]{:S(2)}) collective-permute-start(f32[5,128,128]{2,1,0:T(8,128)S(1)} %slice_add_fusion.11), channel_id=1, source_target_pairs={{0,8},{1,9},{2,10},{3,11},{4,12},{5,13},{6,14},{7,15},{8,0},{9,1},... | collective-permute-start | bytes 983048 | tf_op jit(solution)/shard_map/ppermute | solution.py:14
  72.5 8.0 %collective-permute-start.4 = (f32[4,128,128]{2,1,0:T(8,128)S(1)}, f32[4,128,128]{2,1,0:T(8,128)S(1)}, u32[]{:S(2)}, u32[]{:S(2)}) collective-permute-start(f32[4,128,128]{2,1,0:T(8,128)S(1)} %slice_add_fusion.15), channel_id=1, source_target_pairs={{0,16},{1,17},{2,18},{3,19},{4,20},{5,21},{6,22},{7,23},{8,24},{9,... | collective-permute-start | bytes 786440 | tf_op jit(solution)/shard_map/ppermute | solution.py:14
  80.5 1.5 collective-permute-start.5
  82.0 5.6 %collective-permute-start.6 = (f32[2,128,128]{2,1,0:T(8,128)S(1)}, f32[2,128,128]{2,1,0:T(8,128)S(1)}, u32[]{:S(2)}, u32[]{:S(2)}) collective-permute-start(f32[2,128,128]{2,1,0:T(8,128)S(1)} %slice_add_fusion.23), channel_id=1, source_target_pairs={{0,64},{32,96},{64,0},{96,32},{128,192},{160,224},{192,128},{224,1... | collective-permute-start | bytes 393224 | tf_op jit(solution)/shard_map/ppermute | solution.py:14
  88.3 14.6 %collective-permute-start.7 = (f32[1,128,128]{2,1,0:T(8,128)S(1)}, f32[1,128,128]{2,1,0:T(8,128)S(1)}, u32[]{:S(2)}, u32[]{:S(2)}) collective-permute-start(f32[1,128,128]{2,1,0:T(8,128)S(1)} %get-tuple-element.15), channel_id=1, source_target_pairs={{0,128},{32,160},{64,192},{96,224},{128,0},{160,32},{192,64},{224,... | collective-permute-start | bytes 196616 | tf_op jit(solution)/shard_map/ppermute | solution.py:14
  92.8 10.8 %copy-start.15 = (f32[8]{0:T(128)S(1)}, f32[8]{0:T(128)}, u32[]{:S(2)}) copy-start(f32[8]{0:T(128)} %constant.6.clone) | copy-start | bytes 100
  102.9 5.4 %copy-start.1 = (bf16[8,2048,128]{2,1,0:T(8,128)(2,1)S(1)}, bf16[8,2048,128]{2,1,0:T(8,128)(2,1)}, u32[]{:S(2)}) copy-start(bf16[8,2048,128]{2,1,0:T(8,128)(2,1)} %param.15) | copy-start | bytes 12582916
  108.4 16.9 %copy-start.12 = (bf16[1,2048,128]{2,1,0:T(8,128)(2,1)S(1)}, bf16[1,2048,128]{2,1,0:T(8,128)(2,1)}, u32[]{:S(2)}) copy-start(bf16[1,2048,128]{2,1,0:T(8,128)(2,1)} %copy-done.11) | copy-start | bytes 1572868
  109.1 12.9 %collective-permute-start.8 = (f32[8,128,128]{2,1,0:T(8,128)S(1)}, f32[8,128,128]{2,1,0:T(8,128)S(1)}, u32[]{:S(2)}, u32[]{:S(2)}) collective-permute-start(f32[8,128,128]{2,1,0:T(8,128)S(1)} %convolution_bitcast_fusion.10), channel_id=1, source_target_pairs={{0,1},{1,0},{2,3},{3,2},{4,5},{5,4},{6,7},{7,6},{8,9},{9,8},{10,11... | collective-permute-start | bytes 1572872 | tf_op jit(solution)/shard_map/ppermute | solution.py:14
  109.5 38.9 %copy-start.5 = (bf16[1,2048,128]{2,1,0:T(8,128)(2,1)S(1)}, bf16[1,2048,128]{2,1,0:T(8,128)(2,1)}, u32[]{:S(2)}) copy-start(bf16[1,2048,128]{2,1,0:T(8,128)(2,1)} %copy-done.4) | copy-start | bytes 1572868
  122.1 22.0 %collective-permute-start.9 = (f32[7,128,128]{2,1,0:T(8,128)S(1)}, f32[7,128,128]{2,1,0:T(8,128)S(1)}, u32[]{:S(2)}, u32[]{:S(2)}) collective-permute-start(f32[7,128,128]{2,1,0:T(8,128)S(1)} %slice_add_fusion.2), channel_id=1, source_target_pairs={{0,2},{1,3},{2,0},{3,1},{4,6},{5,7},{6,4},{7,5},{8,10},{9,11},{10,... | collective-permute-start | bytes 1376264 | tf_op jit(solution)/shard_map/ppermute | solution.py:14
  144.2 22.7 %collective-permute-start.10 = (f32[6,128,128]{2,1,0:T(8,128)S(1)}, f32[6,128,128]{2,1,0:T(8,128)S(1)}, u32[]{:S(2)}, u32[]{:S(2)}) collective-permute-start(f32[6,128,128]{2,1,0:T(8,128)S(1)} %slice_add_fusion.6), channel_id=1, source_target_pairs={{0,4},{1,5},{2,6},{3,7},{4,0},{5,1},{6,2},{7,3},{8,12},{9,13},{10,... | collective-permute-start | bytes 1179656 | tf_op jit(solution)/shard_map/ppermute | solution.py:14
  166.9 9.1 %collective-permute-start.11 = (f32[5,128,128]{2,1,0:T(8,128)S(1)}, f32[5,128,128]{2,1,0:T(8,128)S(1)}, u32[]{:S(2)}, u32[]{:S(2)}) collective-permute-start(f32[5,128,128]{2,1,0:T(8,128)S(1)} %slice_add_fusion.10), channel_id=1, source_target_pairs={{0,8},{1,9},{2,10},{3,11},{4,12},{5,13},{6,14},{7,15},{8,0},{9,1},... | collective-permute-start | bytes 983048 | tf_op jit(solution)/shard_map/ppermute | solution.py:14
  176.0 8.3 %collective-permute-start.12 = (f32[4,128,128]{2,1,0:T(8,128)S(1)}, f32[4,128,128]{2,1,0:T(8,128)S(1)}, u32[]{:S(2)}, u32[]{:S(2)}) collective-permute-start(f32[4,128,128]{2,1,0:T(8,128)S(1)} %slice_add_fusion.14), channel_id=1, source_target_pairs={{0,16},{1,17},{2,18},{3,19},{4,20},{5,21},{6,22},{7,23},{8,24},{9,... | collective-permute-start | bytes 786440 | tf_op jit(solution)/shard_map/ppermute | solution.py:14
  184.3 1.5 collective-permute-start.13
  185.9 5.6 %collective-permute-start.14 = (f32[2,128,128]{2,1,0:T(8,128)S(1)}, f32[2,128,128]{2,1,0:T(8,128)S(1)}, u32[]{:S(2)}, u32[]{:S(2)}) collective-permute-start(f32[2,128,128]{2,1,0:T(8,128)S(1)} %slice_add_fusion.22), channel_id=1, source_target_pairs={{0,64},{32,96},{64,0},{96,32},{128,192},{160,224},{192,128},{224,1... | collective-permute-start | bytes 393224 | tf_op jit(solution)/shard_map/ppermute | solution.py:14
  192.1 12.2 %collective-permute-start.15 = (f32[1,128,128]{2,1,0:T(8,128)S(1)}, f32[1,128,128]{2,1,0:T(8,128)S(1)}, u32[]{:S(2)}, u32[]{:S(2)}) collective-permute-start(f32[1,128,128]{2,1,0:T(8,128)S(1)} %get-tuple-element.13), channel_id=1, source_target_pairs={{0,128},{32,160},{64,192},{96,224},{128,0},{160,32},{192,64},{224,... | collective-permute-start | bytes 196616 | tf_op jit(solution)/shard_map/ppermute | solution.py:14
  204.4 5.4 %copy-start.2 = (bf16[8,2048,128]{2,1,0:T(8,128)(2,1)S(1)}, bf16[8,2048,128]{2,1,0:T(8,128)(2,1)}, u32[]{:S(2)}) copy-start(bf16[8,2048,128]{2,1,0:T(8,128)(2,1)} %param.15) | copy-start | bytes 12582916
  209.8 17.5 %copy-start.13 = (bf16[1,2048,128]{2,1,0:T(8,128)(2,1)S(1)}, bf16[1,2048,128]{2,1,0:T(8,128)(2,1)}, u32[]{:S(2)}) copy-start(bf16[1,2048,128]{2,1,0:T(8,128)(2,1)} %copy-done.11) | copy-start | bytes 1572868
  210.5 13.3 %collective-permute-start.16 = (f32[8,128,128]{2,1,0:T(8,128)S(1)}, f32[8,128,128]{2,1,0:T(8,128)S(1)}, u32[]{:S(2)}, u32[]{:S(2)}) collective-permute-start(f32[8,128,128]{2,1,0:T(8,128)S(1)} %convolution_bitcast_fusion.9), channel_id=1, source_target_pairs={{0,1},{1,0},{2,3},{3,2},{4,5},{5,4},{6,7},{7,6},{8,9},{9,8},{10,11... | collective-permute-start | bytes 1572872 | tf_op jit(solution)/shard_map/ppermute | solution.py:14
  210.9 39.6 %copy-start.6 = (bf16[1,2048,128]{2,1,0:T(8,128)(2,1)S(1)}, bf16[1,2048,128]{2,1,0:T(8,128)(2,1)}, u32[]{:S(2)}) copy-start(bf16[1,2048,128]{2,1,0:T(8,128)(2,1)} %copy-done.4) | copy-start | bytes 1572868
  223.9 22.7 %collective-permute-start.17 = (f32[7,128,128]{2,1,0:T(8,128)S(1)}, f32[7,128,128]{2,1,0:T(8,128)S(1)}, u32[]{:S(2)}, u32[]{:S(2)}) collective-permute-start(f32[7,128,128]{2,1,0:T(8,128)S(1)} %slice_add_fusion.1), channel_id=1, source_target_pairs={{0,2},{1,3},{2,0},{3,1},{4,6},{5,7},{6,4},{7,5},{8,10},{9,11},{10,... | collective-permute-start | bytes 1376264 | tf_op jit(solution)/shard_map/ppermute | solution.py:14
  246.6 22.5 %collective-permute-start.18 = (f32[6,128,128]{2,1,0:T(8,128)S(1)}, f32[6,128,128]{2,1,0:T(8,128)S(1)}, u32[]{:S(2)}, u32[]{:S(2)}) collective-permute-start(f32[6,128,128]{2,1,0:T(8,128)S(1)} %slice_add_fusion.5), channel_id=1, source_target_pairs={{0,4},{1,5},{2,6},{3,7},{4,0},{5,1},{6,2},{7,3},{8,12},{9,13},{10,... | collective-permute-start | bytes 1179656 | tf_op jit(solution)/shard_map/ppermute | solution.py:14
  269.2 9.2 %collective-permute-start.19 = (f32[5,128,128]{2,1,0:T(8,128)S(1)}, f32[5,128,128]{2,1,0:T(8,128)S(1)}, u32[]{:S(2)}, u32[]{:S(2)}) collective-permute-start(f32[5,128,128]{2,1,0:T(8,128)S(1)} %slice_add_fusion.9), channel_id=1, source_target_pairs={{0,8},{1,9},{2,10},{3,11},{4,12},{5,13},{6,14},{7,15},{8,0},{9,1},... | collective-permute-start | bytes 983048 | tf_op jit(solution)/shard_map/ppermute | solution.py:14
  278.5 8.4 %collective-permute-start.20 = (f32[4,128,128]{2,1,0:T(8,128)S(1)}, f32[4,128,128]{2,1,0:T(8,128)S(1)}, u32[]{:S(2)}, u32[]{:S(2)}) collective-permute-start(f32[4,128,128]{2,1,0:T(8,128)S(1)} %slice_add_fusion.13), channel_id=1, source_target_pairs={{0,16},{1,17},{2,18},{3,19},{4,20},{5,21},{6,22},{7,23},{8,24},{9,... | collective-permute-start | bytes 786440 | tf_op jit(solution)/shard_map/ppermute | solution.py:14
  286.9 1.5 collective-permute-start.21
  288.5 5.6 %collective-permute-start.22 = (f32[2,128,128]{2,1,0:T(8,128)S(1)}, f32[2,128,128]{2,1,0:T(8,128)S(1)}, u32[]{:S(2)}, u32[]{:S(2)}) collective-permute-start(f32[2,128,128]{2,1,0:T(8,128)S(1)} %slice_add_fusion.21), channel_id=1, source_target_pairs={{0,64},{32,96},{64,0},{96,32},{128,192},{160,224},{192,128},{224,1... | collective-permute-start | bytes 393224 | tf_op jit(solution)/shard_map/ppermute | solution.py:14
  294.7 13.6 %collective-permute-start.23 = (f32[1,128,128]{2,1,0:T(8,128)S(1)}, f32[1,128,128]{2,1,0:T(8,128)S(1)}, u32[]{:S(2)}, u32[]{:S(2)}) collective-permute-start(f32[1,128,128]{2,1,0:T(8,128)S(1)} %get-tuple-element.11), channel_id=1, source_target_pairs={{0,128},{32,160},{64,192},{96,224},{128,0},{160,32},{192,64},{224,... | collective-permute-start | bytes 196616 | tf_op jit(solution)/shard_map/ppermute | solution.py:14
  308.3 5.4 %copy-start.3 = (bf16[8,2048,128]{2,1,0:T(8,128)(2,1)S(1)}, bf16[8,2048,128]{2,1,0:T(8,128)(2,1)}, u32[]{:S(2)}) copy-start(bf16[8,2048,128]{2,1,0:T(8,128)(2,1)} %param.15) | copy-start | bytes 12582916
  313.8 17.3 %copy-start.14 = (bf16[1,2048,128]{2,1,0:T(8,128)(2,1)S(1)}, bf16[1,2048,128]{2,1,0:T(8,128)(2,1)}, u32[]{:S(2)}) copy-start(bf16[1,2048,128]{2,1,0:T(8,128)(2,1)} %copy-done.11) | copy-start | bytes 1572868
  314.5 12.9 %collective-permute-start.24 = (f32[8,128,128]{2,1,0:T(8,128)S(1)}, f32[8,128,128]{2,1,0:T(8,128)S(1)}, u32[]{:S(2)}, u32[]{:S(2)}) collective-permute-start(f32[8,128,128]{2,1,0:T(8,128)S(1)} %convolution_bitcast_fusion.8), channel_id=1, source_target_pairs={{0,1},{1,0},{2,3},{3,2},{4,5},{5,4},{6,7},{7,6},{8,9},{9,8},{10,11... | collective-permute-start | bytes 1572872 | tf_op jit(solution)/shard_map/ppermute | solution.py:14
  314.9 38.6 %copy-start.7 = (bf16[1,2048,128]{2,1,0:T(8,128)(2,1)S(1)}, bf16[1,2048,128]{2,1,0:T(8,128)(2,1)}, u32[]{:S(2)}) copy-start(bf16[1,2048,128]{2,1,0:T(8,128)(2,1)} %copy-done.4) | copy-start | bytes 1572868
  327.5 22.4 %collective-permute-start.25 = (f32[7,128,128]{2,1,0:T(8,128)S(1)}, f32[7,128,128]{2,1,0:T(8,128)S(1)}, u32[]{:S(2)}, u32[]{:S(2)}) collective-permute-start(f32[7,128,128]{2,1,0:T(8,128)S(1)} %slice_add_fusion), channel_id=1, source_target_pairs={{0,2},{1,3},{2,0},{3,1},{4,6},{5,7},{6,4},{7,5},{8,10},{9,11},{10,... | collective-permute-start | bytes 1376264 | tf_op jit(solution)/shard_map/ppermute | solution.py:14
  350.0 22.5 %collective-permute-start.26 = (f32[6,128,128]{2,1,0:T(8,128)S(1)}, f32[6,128,128]{2,1,0:T(8,128)S(1)}, u32[]{:S(2)}, u32[]{:S(2)}) collective-permute-start(f32[6,128,128]{2,1,0:T(8,128)S(1)} %slice_add_fusion.4), channel_id=1, source_target_pairs={{0,4},{1,5},{2,6},{3,7},{4,0},{5,1},{6,2},{7,3},{8,12},{9,13},{10,... | collective-permute-start | bytes 1179656 | tf_op jit(solution)/shard_map/ppermute | solution.py:14
  372.5 9.7 %collective-permute-start.27 = (f32[5,128,128]{2,1,0:T(8,128)S(1)}, f32[5,128,128]{2,1,0:T(8,128)S(1)}, u32[]{:S(2)}, u32[]{:S(2)}) collective-permute-start(f32[5,128,128]{2,1,0:T(8,128)S(1)} %slice_add_fusion.8), channel_id=1, source_target_pairs={{0,8},{1,9},{2,10},{3,11},{4,12},{5,13},{6,14},{7,15},{8,0},{9,1},... | collective-permute-start | bytes 983048 | tf_op jit(solution)/shard_map/ppermute | solution.py:14
  382.3 9.0 %collective-permute-start.28 = (f32[4,128,128]{2,1,0:T(8,128)S(1)}, f32[4,128,128]{2,1,0:T(8,128)S(1)}, u32[]{:S(2)}, u32[]{:S(2)}) collective-permute-start(f32[4,128,128]{2,1,0:T(8,128)S(1)} %slice_add_fusion.12), channel_id=1, source_target_pairs={{0,16},{1,17},{2,18},{3,19},{4,20},{5,21},{6,22},{7,23},{8,24},{9,... | collective-permute-start | bytes 786440 | tf_op jit(solution)/shard_map/ppermute | solution.py:14
  391.3 1.5 collective-permute-start.29
  392.8 5.6 %collective-permute-start.30 = (f32[2,128,128]{2,1,0:T(8,128)S(1)}, f32[2,128,128]{2,1,0:T(8,128)S(1)}, u32[]{:S(2)}, u32[]{:S(2)}) collective-permute-start(f32[2,128,128]{2,1,0:T(8,128)S(1)} %slice_add_fusion.20), channel_id=1, source_target_pairs={{0,64},{32,96},{64,0},{96,32},{128,192},{160,224},{192,128},{224,1... | collective-permute-start | bytes 393224 | tf_op jit(solution)/shard_map/ppermute | solution.py:14
  398.5 12.7 %collective-permute-start.31 = (f32[1,128,128]{2,1,0:T(8,128)S(1)}, f32[1,128,128]{2,1,0:T(8,128)S(1)}, u32[]{:S(2)}, u32[]{:S(2)}) collective-permute-start(f32[1,128,128]{2,1,0:T(8,128)S(1)} %get-tuple-element.9), channel_id=1, source_target_pairs={{0,128},{32,160},{64,192},{96,224},{128,0},{160,32},{192,64},{224,... | collective-permute-start | bytes 196616 | tf_op jit(solution)/shard_map/ppermute | solution.py:14
where the time goes:
time: 417 us; the launch traced here: 416 us
  waiting for transfers between devices  264 us (63%)
  local copies, waits for them, and re-layouts  54.3 us (13%)
  starting transfers between devices  53.5 us (13%)
  matrix products  40.6 us (10%)
    ppermute x32, waiting for transfers between devices, from_partner(): return lax.ppermute(value, axis, pairs)  264 us
    ppermute x32, starting transfers between devices, from_partner(): return lax.ppermute(value, axis, pairs)  53.5 us
    add x8, local copies, waits for them, and re-layouts, apply_operator(): result = result + added.reshape(wide, dev_rows)  20.3 us
    dot_general x4, matrix products, apply_operator(): jnp.einsum('bsr,bcr->cs', u_upper, coefs, preferred_element_type=jnp.floa...  19.4 us
    unnamed x56, local copies, waits for them, and re-layouts  11.7 us
    dot_general x8, matrix products, apply_operator(): jnp.einsum('gsr,gcr->cgs', u_local[level].reshape(groups, node_rows, rank...  10.3 us
    reshape x4, local copies, waits for them, and re-layouts, apply_operator(): result = result + added.reshape(wide, dev_rows)  10.2 us
    transpose x4, local copies, waits for them, and re-layouts, apply_operator(): jnp.einsum('gsr,gcr->cgs', u_local[level].reshape(groups, node_rows, rank...  10.1 us
  transfers between devices with their start and end apart: 32, of which 28 were waited for; matrix products, arithmetic and copies ran while one was open for 16% of the time, Pallas kernels for 0%

commit v1 on v0

--- a/solution.py
+++ b/solution.py
@@ -6,32 +6,21 @@
 from jax.sharding import PartitionSpec as P
 
 ITERS = 4
+AXES = ("hi", "lo")
 
 
-def from_partner(value, axis, distance):
-    mask = 2**distance
-    pairs = [(source, source ^ mask) for source in range(lax.axis_size(axis))]
-    return lax.ppermute(value, axis, pairs)
-
-
-def lower_steps(stack, lo_bits):
-    found = []
-    carried = stack
-    for level_bit in range(lo_bits):
-        arrived = from_partner(carried, "lo", level_bit)
-        found.append(arrived[0])
-        carried = carried[1:] + arrived[1:]
-    return (found, carried)
-
-
-def upper_sums(hi_parts, hi_bits):
-    found = []
-    carried = hi_parts
-    for level_bit in range(hi_bits):
-        arrived = from_partner(carried, "hi", level_bit)
-        found.append(arrived[0])
-        carried = carried[1:] + arrived[1:]
-    return found
+def sibling_sums(parts):
+    levels, wide, rank_cols = parts.shape
+    count = lax.axis_size("hi") * lax.axis_size("lo")
+    slice_rows = levels * wide // count
+    gathered = lax.all_to_all(parts.reshape(count, slice_rows, rank_cols), AXES, 0, 0)
+    me = lax.axis_index("hi") * lax.axis_size("lo") + lax.axis_index("lo")
+    level = me * slice_rows // wide
+    rows = lax.broadcasted_iota(jnp.int32, (count, count), 0)
+    cols = lax.broadcasted_iota(jnp.int32, (count, count), 1)
+    sibling = (lax.shift_right_logical(rows ^ cols, level) == 1).astype(jnp.float32)
+    sums = jnp.einsum("ds,sir->dir", sibling, gathered, precision=lax.Precision.HIGHEST)
+    return lax.all_to_all(sums, AXES, 0, 0).reshape(levels, wide, rank_cols)
 
 
 def apply_operator(state, leaves, u_local, v_local, u_upper, v_upper):
@@ -40,11 +29,9 @@
     local_count = u_local.shape[0]
     upper_count = u_upper.shape[0]
     level_count = local_count + upper_count
-    lo_bits = lax.axis_size("lo").bit_length() - 1
-    hi_bits = lax.axis_size("hi").bit_length() - 1
     rank_cols = u_local.shape[2]
     parts = jnp.einsum("bsr,cs->bcr", v_upper, state, preferred_element_type=jnp.float32)
-    lower_found, hi_parts = lower_steps(parts, lo_bits)
+    found = sibling_sums(parts)
     blocks = leaves.reshape(dev_rows // leaf_rows, leaf_rows, leaf_rows)
     result = jnp.einsum(
         "gij,cgj->cgi",
@@ -72,8 +59,6 @@
             preferred_element_type=jnp.float32,
         )
         result = result + added.reshape(wide, dev_rows)
-    upper_found = upper_sums(hi_parts, hi_bits)
-    coefs = jnp.stack(lower_found + upper_found)
     factors = jnp.array(
         [
             1.0 / math.sqrt(dev_rows * 2**level_bit * level_count)
@@ -81,7 +66,7 @@
         ],
         dtype=jnp.float32,
     )
-    coefs = (coefs * factors[:, None, None]).astype(jnp.bfloat16)
+    coefs = (found * factors[:, None, None]).astype(jnp.bfloat16)
     result = result + jnp.einsum("bsr,bcr->cs", u_upper, coefs, preferred_element_type=jnp.float32)
     return result.astype(jnp.bfloat16)
 

time: 417 us -> 285 us (0.68)
  waiting for transfers between devices: 264 us -> 77.5 us
  starting transfers between devices: 53.5 us -> 86.3 us
  matrix products: 40.6 us -> 62.6 us
  local copies, waits for them, and re-layouts: 54.3 us -> 48.3 us
    ppermute x32 -> x0, waiting for transfers between devices: 264 us -> none  [from_partner(): return lax.ppermute(value, axis, pairs)]
    all_to_all x0 -> x8, starting transfers between devices: none -> 86.3 us  [the longest x4 51.9 us: sibling_sums(): lax.all_to_all(parts.reshape(count, slice_rows, rank_cols), AXES, 0, 0)]
    all_to_all x0 -> x8, waiting for transfers between devices: none -> 77.5 us  [the longest x4 65.2 us: sibling_sums(): lax.all_to_all(parts.reshape(count, slice_rows, rank_cols), AXES, 0, 0)]
    ppermute x32 -> x0, starting transfers between devices: 53.5 us -> none  [from_partner(): return lax.ppermute(value, axis, pairs)]
    unnamed x56 -> x24, local copies, waits for them, and re-layouts: 11.7 us -> 0.05 us
    dot_general x8, matrix products: 2.3 us -> 11.3 us  [apply_operator(): jnp.einsum('gsr,cgs->gcr', v_local[level].reshape(groups, node_rows, rank...]
    dot_general x0 -> x4, matrix products: none -> 5.97 us  [sibling_sums(): jnp.einsum('ds,sir->dir', sibling, gathered, precision=lax.Precision.HIGH...]
    convert_element_type x0 -> x4, other arithmetic: none -> 5.05 us  [apply_operator(): coefs = (found * factors[:, None, None]).astype(jnp.bfloat16)]
  transfers between devices with their start and end apart: 32 -> 8, of which waited for: 28 -> 8; matrix products, arithmetic and copies ran while one was open for 16% -> 26% of each run, Pallas kernels for 0% -> 0%
where the time goes in v1:
time: 285 us; the launch traced here: 280 us
  starting transfers between devices  86.3 us (30%)
  waiting for transfers between devices  77.5 us (27%)
  matrix products  62.6 us (22%)
  local copies, waits for them, and re-layouts  48.3 us (17%)
  other arithmetic  5.25 us (2%)
    all_to_all x4, waiting for transfers between devices, sibling_sums(): lax.all_to_all(parts.reshape(count, slice_rows, rank_cols), AXES, 0, 0)  65.2 us
    all_to_all x4, starting transfers between devices, sibling_sums(): lax.all_to_all(parts.reshape(count, slice_rows, rank_cols), AXES, 0, 0)  51.9 us
    all_to_all x4, starting transfers between devices, sibling_sums(): return lax.all_to_all(sums, AXES, 0, 0).reshape(levels, wide, rank_cols)  34.4 us
    add x8, local copies, waits for them, and re-layouts, apply_operator(): result = result + added.reshape(wide, dev_rows)  19.3 us
    dot_general x4, matrix products, apply_operator(): jnp.einsum('bsr,bcr->cs', u_upper, coefs, preferred_element_type=jnp.floa...  17.9 us
    all_to_all x4, waiting for transfers between devices, sibling_sums(): return lax.all_to_all(sums, AXES, 0, 0).reshape(levels, wide, rank_cols)  12.2 us
    dot_general x8, matrix products, apply_operator(): jnp.einsum('gsr,gcr->cgs', u_local[level].reshape(groups, node_rows, rank...  11.6 us
    dot_general x8, matrix products, apply_operator(): jnp.einsum('gsr,cgs->gcr', v_local[level].reshape(groups, node_rows, rank...  11.3 us
  transfers between devices with their start and end apart: 8, of which 8 were waited for; matrix products, arithmetic and copies ran while one was open for 26% of the time, Pallas kernels for 0%

profile of v1, /device:TPU:6, one launch (start us, length us, event | category | flops | bytes accessed | tf_op | source)
XLA Modules:
  0.0 280.3 jit_solution(6382130513625310506)
XLA Ops:
  0.0 4.0 %fusion.50 = f32[128,8,128]{2,0,1:T(8,128)} fusion(bf16[8,2048,128]{2,1,0:T(8,128)(2,1)} %param.15, bf16[128,2048]{1,0:T(8,128)(2,1)} %param.10), kind=kOutput, calls=%fused_computation.66 | convolution fusion | flops 536870912 | bytes 5242880 | tf_op jit(solution)/shard_map/bsr,cs->bcr/dot_general | solution.py:33
  4.0 15.6 %all-to-all-start = ((f32[256,4,128]{2,1,0:T(4,128)}), f32[256,4,128]{2,1,0:T(4,128)}, u32[]{:S(2)}, u32[]{:S(2)}) async-start(f32[256,4,128]{2,1,0:T(4,128)} %bitcast.14), calls=%async_computation | async-start | bytes 1048576 | tf_op jit(solution)/shard_map/all_to_all | solution.py:16
  19.7 1.8 fusion.38
  21.5 2.1 fusion.81
  23.5 2.1 fusion.82
  25.6 13.0 %all-to-all-done = f32[256,4,128]{2,1,0:T(4,128)} async-done(((f32[256,4,128]{2,1,0:T(4,128)}), f32[256,4,128]{2,1,0:T(4,128)}, u32[]{:S(2)}, u32[]{:S(2)}) %all-to-all-start) | async-done | bytes 524320 | tf_op jit(solution)/shard_map/all_to_all | solution.py:16
  38.6 1.5 fusion.58
  41.2 8.6 %all-to-all-start.1 = ((f32[256,4,128]{2,1,0:T(4,128)}), f32[256,4,128]{2,1,0:T(4,128)}, u32[]{:S(2)}, u32[]{:S(2)}) async-start(f32[256,4,128]{2,1,0:T(4,128)} %copy.63), calls=%async_computation.1 | async-start | bytes 1048576 | tf_op jit(solution)/shard_map/all_to_all | solution.py:23
  49.8 1.3 fusion.36
  51.2 2.7 fusion.11
  53.9 2.5 copy.57
  56.4 2.6 copy.60
  59.0 1.5 fusion.33
  61.7 2.5 copy.59
  64.3 2.5 copy.61
  66.8 2.1 all-to-all-done.1
  68.9 1.3 fusion.49
  70.2 4.4 %fusion.7 = bf16[128,2048]{1,0:T(8,128)(2,1)S(1)} fusion(bf16[8,128,128]{2,1,0:T(8,128)(2,1)S(1)} %fusion.49, bf16[8,2048,128]{2,1,0:T(8,128)(2,1)} %param.14, f32[128,2048]{1,0:T(8,128)} %copy.60, f32[128,2048]{1,0:T(8,128)} %copy.61), kind=kOutput, calls=%fused_computation.11 | convolution fusion | flops 537657344 | bytes 7077888 | tf_op jit(solution)/shard_map/bsr,bcr->cs/dot_general | solution.py:70
  74.6 1.5 fusion.47
  76.1 12.7 %all-to-all-start.2 = ((f32[256,4,128]{2,1,0:T(4,128)}), f32[256,4,128]{2,1,0:T(4,128)}, u32[]{:S(2)}, u32[]{:S(2)}) async-start(f32[256,4,128]{2,1,0:T(4,128)} %bitcast.228), calls=%async_computation.2 | async-start | bytes 1048576 | tf_op jit(solution)/shard_map/all_to_all | solution.py:16
  88.8 1.5 fusion.26
  90.4 17.4 %all-to-all-done.2 = f32[256,4,128]{2,1,0:T(4,128)} async-done(((f32[256,4,128]{2,1,0:T(4,128)}), f32[256,4,128]{2,1,0:T(4,128)}, u32[]{:S(2)}, u32[]{:S(2)}) %all-to-all-start.2) | async-done | bytes 524320 | tf_op jit(solution)/shard_map/all_to_all | solution.py:16
  107.8 1.5 fusion.56
  110.4 8.6 %all-to-all-start.3 = ((f32[256,4,128]{2,1,0:T(4,128)}), f32[256,4,128]{2,1,0:T(4,128)}, u32[]{:S(2)}, u32[]{:S(2)}) async-start(f32[256,4,128]{2,1,0:T(4,128)} %copy.72), calls=%async_computation.3 | async-start | bytes 1048576 | tf_op jit(solution)/shard_map/all_to_all | solution.py:23
  119.0 1.3 convolution_bitcast_fusion.6
  120.3 2.5 copy.68
  122.8 2.6 copy.70
  125.4 1.4 fusion.29
  126.8 1.8 fusion.31
  129.9 2.5 copy.66
  132.5 2.5 copy.69
  135.0 3.1 %all-to-all-done.3 = f32[256,4,128]{2,1,0:T(4,128)} async-done(((f32[256,4,128]{2,1,0:T(4,128)}), f32[256,4,128]{2,1,0:T(4,128)}, u32[]{:S(2)}, u32[]{:S(2)}) %all-to-all-start.3) | async-done | bytes 524320 | tf_op jit(solution)/shard_map/all_to_all | solution.py:23
  138.1 1.3 fusion.46
  139.4 4.4 %fusion.6 = bf16[128,2048]{1,0:T(8,128)(2,1)S(1)} fusion(bf16[8,128,128]{2,1,0:T(8,128)(2,1)S(1)} %fusion.46, bf16[8,2048,128]{2,1,0:T(8,128)(2,1)} %param.14, f32[128,2048]{1,0:T(8,128)} %copy.69, f32[128,2048]{1,0:T(8,128)} %copy.70), kind=kOutput, calls=%fused_computation.10 | convolution fusion | flops 537657344 | bytes 7077888 | tf_op jit(solution)/shard_map/bsr,bcr->cs/dot_general | solution.py:70
  143.8 1.5 fusion.44
  145.3 11.7 %all-to-all-start.4 = ((f32[256,4,128]{2,1,0:T(4,128)}), f32[256,4,128]{2,1,0:T(4,128)}, u32[]{:S(2)}, u32[]{:S(2)}) async-start(f32[256,4,128]{2,1,0:T(4,128)} %bitcast.229), calls=%async_computation.4 | async-start | bytes 1048576 | tf_op jit(solution)/shard_map/all_to_all | solution.py:16
  157.0 1.5 fusion.19
  158.5 17.4 %all-to-all-done.4 = f32[256,4,128]{2,1,0:T(4,128)} async-done(((f32[256,4,128]{2,1,0:T(4,128)}), f32[256,4,128]{2,1,0:T(4,128)}, u32[]{:S(2)}, u32[]{:S(2)}) %all-to-all-start.4) | async-done | bytes 524320 | tf_op jit(solution)/shard_map/all_to_all | solution.py:16
  176.0 1.5 fusion.54
  178.6 8.6 %all-to-all-start.5 = ((f32[256,4,128]{2,1,0:T(4,128)}), f32[256,4,128]{2,1,0:T(4,128)}, u32[]{:S(2)}, u32[]{:S(2)}) async-start(f32[256,4,128]{2,1,0:T(4,128)} %copy.81), calls=%async_computation.5 | async-start | bytes 1048576 | tf_op jit(solution)/shard_map/all_to_all | solution.py:23
  187.2 1.3 convolution_bitcast_fusion.5
  188.5 2.5 copy.77
  191.0 2.6 copy.79
  193.6 1.4 fusion.22
  195.0 1.9 fusion.24
  198.1 2.5 copy.75
  200.7 2.5 copy.78
  203.2 3.1 %all-to-all-done.5 = f32[256,4,128]{2,1,0:T(4,128)} async-done(((f32[256,4,128]{2,1,0:T(4,128)}), f32[256,4,128]{2,1,0:T(4,128)}, u32[]{:S(2)}, u32[]{:S(2)}) %all-to-all-start.5) | async-done | bytes 524320 | tf_op jit(solution)/shard_map/all_to_all | solution.py:23
  206.2 1.3 fusion.43
  207.6 4.4 %fusion.5 = bf16[128,2048]{1,0:T(8,128)(2,1)S(1)} fusion(bf16[8,128,128]{2,1,0:T(8,128)(2,1)S(1)} %fusion.43, bf16[8,2048,128]{2,1,0:T(8,128)(2,1)} %param.14, f32[128,2048]{1,0:T(8,128)} %copy.78, f32[128,2048]{1,0:T(8,128)} %copy.79), kind=kOutput, calls=%fused_computation.9 | convolution fusion | flops 537657344 | bytes 7077888 | tf_op jit(solution)/shard_map/bsr,bcr->cs/dot_general | solution.py:70
  212.0 1.5 fusion.41
  213.5 11.8 %all-to-all-start.6 = ((f32[256,4,128]{2,1,0:T(4,128)}), f32[256,4,128]{2,1,0:T(4,128)}, u32[]{:S(2)}, u32[]{:S(2)}) async-start(f32[256,4,128]{2,1,0:T(4,128)} %bitcast.227), calls=%async_computation.6 | async-start | bytes 1048576 | tf_op jit(solution)/shard_map/all_to_all | solution.py:16
  225.2 1.5 fusion.12
  226.7 17.4 %all-to-all-done.6 = f32[256,4,128]{2,1,0:T(4,128)} async-done(((f32[256,4,128]{2,1,0:T(4,128)}), f32[256,4,128]{2,1,0:T(4,128)}, u32[]{:S(2)}, u32[]{:S(2)}) %all-to-all-start.6) | async-done | bytes 524320 | tf_op jit(solution)/shard_map/all_to_all | solution.py:16
  244.2 1.5 fusion.52
  246.8 8.6 %all-to-all-start.7 = ((f32[256,4,128]{2,1,0:T(4,128)}), f32[256,4,128]{2,1,0:T(4,128)}, u32[]{:S(2)}, u32[]{:S(2)}) async-start(f32[256,4,128]{2,1,0:T(4,128)} %copy.90), calls=%async_computation.7 | async-start | bytes 1048576 | tf_op jit(solution)/shard_map/all_to_all | solution.py:23
  256.7 2.5 copy.86
  259.2 2.6 copy.88
  261.8 1.3 fusion.15
  263.2 1.8 fusion.17
  266.3 2.5 copy.84
  268.8 1.6 copy.87
  270.4 4.0 %all-to-all-done.7 = f32[256,4,128]{2,1,0:T(4,128)} async-done(((f32[256,4,128]{2,1,0:T(4,128)}), f32[256,4,128]{2,1,0:T(4,128)}, u32[]{:S(2)}, u32[]{:S(2)}) %all-to-all-start.7) | async-done | bytes 524320 | tf_op jit(solution)/shard_map/all_to_all | solution.py:23
  275.6 4.8 %fusion.4 = bf16[128,2048]{1,0:T(8,128)(2,1)} fusion(bf16[8,128,128]{2,1,0:T(8,128)(2,1)S(1)} %fusion.40, bf16[8,2048,128]{2,1,0:T(8,128)(2,1)} %param.14, f32[128,2048]{1,0:T(8,128)S(1)} %copy.87, f32[128,2048]{1,0:T(8,128)} %copy.88), kind=kOutput, calls=%fused_computation.8 | convolution fusion | flops 537657344 | bytes 7077888 | tf_op jit(solution)/shard_map/bsr,bcr->cs/dot_general | solution.py:70
  (42 shorter events, 12.2 us)
Async XLA Ops:
  0.0 19.7 %copy-start = (bf16[2048,512]{1,0:T(8,128)(2,1)S(1)}, bf16[2048,512]{1,0:T(8,128)(2,1)}, u32[]{:S(2)}) copy-start(bf16[2048,512]{1,0:T(8,128)(2,1)} %param.11) | copy-start | bytes 6291460
  0.0 19.7 %copy-start.10 = (bf16[128,2048]{1,0:T(8,128)(2,1)S(1)}, bf16[128,2048]{1,0:T(8,128)(2,1)}, u32[]{:S(2)}) copy-start(bf16[128,2048]{1,0:T(8,128)(2,1)} %param.10) | copy-start | bytes 1572868
  4.0 34.6 %all-to-all-start = ((f32[256,4,128]{2,1,0:T(4,128)}), f32[256,4,128]{2,1,0:T(4,128)}, u32[]{:S(2)}, u32[]{:S(2)}) async-start(f32[256,4,128]{2,1,0:T(4,128)} %bitcast.14), calls=%async_computation | async-start | bytes 1048576 | tf_op jit(solution)/shard_map/all_to_all | solution.py:16
  41.2 27.6 %all-to-all-start.1 = ((f32[256,4,128]{2,1,0:T(4,128)}), f32[256,4,128]{2,1,0:T(4,128)}, u32[]{:S(2)}, u32[]{:S(2)}) async-start(f32[256,4,128]{2,1,0:T(4,128)} %copy.63), calls=%async_computation.1 | async-start | bytes 1048576 | tf_op jit(solution)/shard_map/all_to_all | solution.py:23
  56.4 12.5 %copy-start.11 = (f32[8]{0:T(128)S(1)}, f32[8]{0:T(128)}, u32[]{:S(2)}) copy-start(f32[8]{0:T(128)} %constant.42.clone) | copy-start | bytes 100
  68.9 5.7 %copy-start.1 = (bf16[8,2048,128]{2,1,0:T(8,128)(2,1)S(1)}, bf16[8,2048,128]{2,1,0:T(8,128)(2,1)}, u32[]{:S(2)}) copy-start(bf16[8,2048,128]{2,1,0:T(8,128)(2,1)} %param.15) | copy-start | bytes 12582916
  74.6 1.5 copy-start.8
  76.1 31.7 %all-to-all-start.2 = ((f32[256,4,128]{2,1,0:T(4,128)}), f32[256,4,128]{2,1,0:T(4,128)}, u32[]{:S(2)}, u32[]{:S(2)}) async-start(f32[256,4,128]{2,1,0:T(4,128)} %bitcast.228), calls=%async_computation.2 | async-start | bytes 1048576 | tf_op jit(solution)/shard_map/all_to_all | solution.py:16
  110.4 27.6 %all-to-all-start.3 = ((f32[256,4,128]{2,1,0:T(4,128)}), f32[256,4,128]{2,1,0:T(4,128)}, u32[]{:S(2)}, u32[]{:S(2)}) async-start(f32[256,4,128]{2,1,0:T(4,128)} %copy.72), calls=%async_computation.3 | async-start | bytes 1048576 | tf_op jit(solution)/shard_map/all_to_all | solution.py:23
  125.4 3.3 %copy-start.4 = (bf16[1,2048,128]{2,1,0:T(8,128)(2,1)S(1)}, bf16[1,2048,128]{2,1,0:T(8,128)(2,1)}, u32[]{:S(2)}) copy-start(bf16[1,2048,128]{2,1,0:T(8,128)(2,1)} %get-tuple-element.6) | copy-start | bytes 1572868
  138.1 5.7 %copy-start.2 = (bf16[8,2048,128]{2,1,0:T(8,128)(2,1)S(1)}, bf16[8,2048,128]{2,1,0:T(8,128)(2,1)}, u32[]{:S(2)}) copy-start(bf16[8,2048,128]{2,1,0:T(8,128)(2,1)} %param.15) | copy-start | bytes 12582916
  143.8 1.5 copy-start.9
  145.3 30.7 %all-to-all-start.4 = ((f32[256,4,128]{2,1,0:T(4,128)}), f32[256,4,128]{2,1,0:T(4,128)}, u32[]{:S(2)}, u32[]{:S(2)}) async-start(f32[256,4,128]{2,1,0:T(4,128)} %bitcast.229), calls=%async_computation.4 | async-start | bytes 1048576 | tf_op jit(solution)/shard_map/all_to_all | solution.py:16
  178.6 27.6 %all-to-all-start.5 = ((f32[256,4,128]{2,1,0:T(4,128)}), f32[256,4,128]{2,1,0:T(4,128)}, u32[]{:S(2)}, u32[]{:S(2)}) async-start(f32[256,4,128]{2,1,0:T(4,128)} %copy.81), calls=%async_computation.5 | async-start | bytes 1048576 | tf_op jit(solution)/shard_map/all_to_all | solution.py:23
  193.6 3.3 %copy-start.5 = (bf16[1,2048,128]{2,1,0:T(8,128)(2,1)S(1)}, bf16[1,2048,128]{2,1,0:T(8,128)(2,1)}, u32[]{:S(2)}) copy-start(bf16[1,2048,128]{2,1,0:T(8,128)(2,1)} %get-tuple-element.6) | copy-start | bytes 1572868
  206.2 5.7 %copy-start.3 = (bf16[8,2048,128]{2,1,0:T(8,128)(2,1)S(1)}, bf16[8,2048,128]{2,1,0:T(8,128)(2,1)}, u32[]{:S(2)}) copy-start(bf16[8,2048,128]{2,1,0:T(8,128)(2,1)} %param.15) | copy-start | bytes 12582916
  211.9 1.5 copy-start.7
  213.5 30.7 %all-to-all-start.6 = ((f32[256,4,128]{2,1,0:T(4,128)}), f32[256,4,128]{2,1,0:T(4,128)}, u32[]{:S(2)}, u32[]{:S(2)}) async-start(f32[256,4,128]{2,1,0:T(4,128)} %bitcast.227), calls=%async_computation.6 | async-start | bytes 1048576 | tf_op jit(solution)/shard_map/all_to_all | solution.py:16
  246.8 27.6 %all-to-all-start.7 = ((f32[256,4,128]{2,1,0:T(4,128)}), f32[256,4,128]{2,1,0:T(4,128)}, u32[]{:S(2)}, u32[]{:S(2)}) async-start(f32[256,4,128]{2,1,0:T(4,128)} %copy.90), calls=%async_computation.7 | async-start | bytes 1048576 | tf_op jit(solution)/shard_map/all_to_all | solution.py:23
  259.2 5.8 %copy-start.6 = (bf16[1,2048,128]{2,1,0:T(8,128)(2,1)S(1)}, bf16[1,2048,128]{2,1,0:T(8,128)(2,1)}, u32[]{:S(2)}) copy-start(bf16[1,2048,128]{2,1,0:T(8,128)(2,1)} %get-tuple-element.6) | copy-start | bytes 1572868
